TPU v7x, 128 devices: a whole 4x4x4 slice. The times are simulated.
128 devices in a mesh: group: 4 (over z), shard: 32 (over x, y, core).
Axes of the slice: x: 4, y: 4, z: 4, core: 2. Of those that a mesh axis runs over, the one named last changes fastest.
Arguments:
- vectors: float32 [16384, 256], P(('group', 'shard')), may hold values from -160 to 160
- item_codes: int32 [16384], P(('group', 'shard')), may hold values from 0 to 63, as said below
- coarse_book: float32 [64, 256], replicated, may hold values from -24 to 24
- fine_books: float32 [8, 16384, 256], P('group', 'shard'), may hold values from -2 to 2
Outputs:
- item_grad: float32 [16384, 256], P(('group', 'shard'))
- fine_grad: float32 [8, 16384, 256], P('group', 'shard')
- coarse_grad: float32 [64, 256], replicated
Inputs may be any that keep to these rules, and one draw needn't show every extreme that they name: `item_codes`: the items of one device fall into one group at most 32 times, and one group receives exactly 32 items from every device.
All inputs are finite; a program needn't handle non-finite values.
Results may differ from a plain program's by a relative error of at most 0.0003.
Values sent between devices are 32-bit elements; how exact they have to be, the bound alone decides.
No kernel may reach another device: no remote copies, remote signals or barrier semaphores. Data moves between devices by JAX's collectives and lax.ppermute only.
A program may use at most 192 MiB of HBM per device.

v0:
```python
import jax
import jax.numpy as jnp
from jax import lax
from jax.sharding import PartitionSpec as P

sharpness = 2.5
highest = lax.Precision.HIGHEST


def contract(former, latter, former_dim, latter_dim):
    return lax.dot_general(
        former,
        latter,
        (((former_dim,), (latter_dim,)), ((), ())),
        precision=highest,
        preferred_element_type=jnp.float32,
    )


def per_device(vectors, item_codes, coarse_book, fine_books):
    local_groups, book_rows, feature_count = fine_books.shape
    group_count = lax.axis_size("group")
    total_groups = local_groups * group_count
    coarse_total = coarse_book.shape[0]
    per_group = coarse_total // total_groups
    item_count = vectors.shape[0]
    slot_size = item_count // 4
    slot_total = local_groups * group_count * slot_size
    onehot = (item_codes[:, None] == jnp.arange(coarse_total, dtype=jnp.int32)[None, :]).astype(
        jnp.float32
    )
    residual = vectors - contract(onehot, coarse_book, 1, 0)
    group_of = item_codes // per_group
    member = (group_of[:, None] == jnp.arange(total_groups, dtype=jnp.int32)[None, :]).astype(
        jnp.int32
    )
    position = jnp.sum((jnp.cumsum(member, axis=0) - 1) * member, axis=1)
    target = (
        group_of % local_groups * group_count + group_of // local_groups
    ) * slot_size + position
    placing = (jnp.arange(slot_total, dtype=jnp.int32)[:, None] == target[None, :]).astype(
        jnp.float32
    )
    outgoing = contract(placing, residual, 1, 0).reshape(
        local_groups, group_count, slot_size, feature_count
    )
    occupied = jnp.sum(placing, axis=1).reshape(local_groups, group_count, slot_size)
    arrived, arrived_mask = (
        lax.all_to_all(outgoing, "group", split_axis=1, concat_axis=1, tiled=True),
        lax.all_to_all(occupied, "group", split_axis=1, concat_axis=1, tiled=True),
    )
    own_count = group_count * slot_size
    own_rows = arrived.reshape(local_groups, own_count, feature_count)
    own_live = arrived_mask.reshape(local_groups, own_count)
    row_grads = []
    book_grads = []
    spread_rows, spread_mask = (
        lax.all_gather(arrived, "shard", axis=1, tiled=True),
        lax.all_gather(arrived_mask, "shard", axis=1, tiled=True),
    )
    row_total = spread_rows.shape[1] * slot_size
    all_rows = spread_rows.reshape(local_groups, row_total, feature_count)
    for book_index in range(local_groups):
        codebook = fine_books[book_index]
        entries = all_rows[book_index]
        scores = sharpness * contract(entries, codebook, 1, 1)
        peak_score = lax.pmax(jnp.max(scores, axis=1), "shard")
        weights = jnp.exp(scores - peak_score[:, None])
        partial_total = jnp.sum(weights, axis=1)
        partial_quant = contract(weights, codebook, 1, 0)
        quant_sum, denominator_own = (
            lax.psum_scatter(partial_quant, "shard", scatter_dimension=0, tiled=True),
            lax.psum_scatter(partial_total, "shard", scatter_dimension=0, tiled=True),
        )
        quantized = quant_sum / denominator_own[:, None]
        own_error = (quantized - own_rows[book_index]) * own_live[book_index][:, None]
        own_inner = jnp.sum(own_error * quantized, axis=1)
        error_rows, inner_term, denominator = (
            lax.all_gather(own_error, "shard", axis=0, tiled=True),
            lax.all_gather(own_inner, "shard", axis=0, tiled=True),
            lax.all_gather(denominator_own, "shard", axis=0, tiled=True),
        )
        probability = weights / denominator[:, None]
        alignment = contract(error_rows, codebook, 1, 1)
        slopes = probability * (alignment - inner_term[:, None])
        pushed = sharpness * contract(slopes, codebook, 1, 0)
        back_sum = lax.psum_scatter(pushed, "shard", scatter_dimension=0, tiled=True)
        row_grads.append(back_sum - own_error)
        book_grads.append(
            contract(probability, error_rows, 0, 0) + sharpness * contract(slopes, entries, 0, 0)
        )
    fine_grad = jnp.stack(book_grads)
    returned = jnp.stack(row_grads).reshape(local_groups, group_count, slot_size, feature_count)
    homeward = lax.all_to_all(returned, "group", split_axis=1, concat_axis=1, tiled=True)
    item_grad = contract(placing, homeward.reshape(slot_total, feature_count), 0, 0)
    coarse_grad = lax.psum(-contract(onehot, item_grad, 0, 0), ("group", "shard"))
    return (item_grad, fine_grad, coarse_grad)


def solution(mesh):
    placed = (P(("group", "shard"), None), P(("group", "shard")), P(), P("group", "shard", None))
    return jax.shard_map(
        per_device,
        mesh=mesh,
        in_specs=placed,
        out_specs=(P(("group", "shard"), None), P("group", "shard", None), P()),
        check_vma=False,
    )
```

profile of v0, /device:TPU:1, one launch (start us, length us, event | category | flops | bytes accessed | tf_op | source)
XLA Modules:
  0.0 839.8 jit_solution(5621896040765602508)
XLA Ops:
  10.5 11.3 %all_to_all.15 = f32[2,4,32,256]{3,2,0,1:T(8,128)} all-to-all(f32[2,4,32,256]{3,2,0,1:T(8,128)S(1)} %copy.28), channel_id=1, replica_groups=mesh['group'=4,'shard'=32] {'group'}, dimensions={1} | all-to-all | bytes 524288 | tf_op jit(solution)/shard_map/all_to_all | solution.py:49
  21.9 54.1 %all-gather.8.cloned.1.call-done = f32[2,128,32,256]{3,2,0,1:T(8,128)} async-done(((f32[2,4,32,256]{3,2,0,1:T(8,128)}), f32[2,128,32,256]{3,2,0,1:T(8,128)}) %all-gather.8.cloned.1.call-update) | async-done | bytes 8388624 | tf_op jit(solution)/shard_map/all_gather | solution.py:58
  76.0 4.4 fusion.61
  80.4 9.2 %multiply_reduce_fusion = (f32[4096]{0:T(1024)S(1)}, f32[4096,512]{0,1:T(8,128)}) fusion(f32[4096,256]{1,0:T(8,128)S(1)} %bitcast.75, f32[2,512,256]{2,1,0:T(8,128)S(1)} %copy-done.8), kind=kOutput, calls=%fused_computation.4 | convolution fusion | flops 6446641152 | bytes 13123584 | tf_op jit(solution)/shard_map/dot_general | solution.py:11
  89.6 9.2 %multiply_reduce_fusion.1 = (f32[4096]{0:T(1024)S(1)}, f32[4096,512]{0,1:T(8,128)}) fusion(f32[4096,256]{1,0:T(8,128)S(1)} %bitcast.77, f32[2,512,256]{2,1,0:T(8,128)S(1)} %copy-done.8), kind=kOutput, calls=%fused_computation.5 | convolution fusion | flops 6446641152 | bytes 13123584 | tf_op jit(solution)/shard_map/dot_general | solution.py:11
  98.8 121.3 %all-reduce.3 = (f32[4096]{0:T(1024)S(1)}, f32[4096]{0:T(1024)S(1)}) all-reduce(f32[4096]{0:T(1024)S(1)} %get-tuple-element.17, f32[4096]{0:T(1024)S(1)} %get-tuple-element.19), channel_id=1, replica_groups=mesh['group'=4,'shard'=32] {'shard'}, use_global_device_ids=true, to_apply=%region_11.12 | all-reduce | flops 8192 | bytes 65536 | tf_op jit(solution)/shard_map/pmax | solution.py:67
  220.2 17.2 %fusion = f32[4096,256]{1,0:T(8,128)} fusion(f32[4096,512]{0,1:T(8,128)} %get-tuple-element.20, f32[4096]{0:T(1024)S(1)} %get-tuple-element.8, f32[2,512,256]{2,1,0:T(8,128)S(1)} %copy-done.8), kind=kOutput, calls=%fused_computation.8 | convolution fusion | flops 6446645248 | bytes 13123584 | tf_op jit(solution)/shard_map/dot_general | solution.py:11
  237.6 17.2 %fusion.3 = f32[4096,256]{1,0:T(8,128)} fusion(f32[4096,512]{0,1:T(8,128)} %get-tuple-element.18, f32[4096]{0:T(1024)S(1)} %get-tuple-element.7, f32[2,512,256]{2,1,0:T(8,128)S(1)} %copy-done.8), kind=kOutput, calls=%fused_computation.11 | convolution fusion | flops 6446645248 | bytes 13123584 | tf_op jit(solution)/shard_map/dot_general | solution.py:11
  255.7 4.1 all-to-all-start.1
  264.1 5.0 fusion.2
  269.1 5.0 fusion.5
  274.1 125.5 %all-reduce.2 = (f32[4096]{0:T(1024)S(1)}, f32[4096]{0:T(1024)S(1)}) all-reduce(f32[4096]{0:T(1024)S(1)} %fusion.5, f32[4096]{0:T(1024)S(1)} %fusion.2), channel_id=5, replica_groups=mesh['group'=4,'shard'=32] {'shard'}, use_global_device_ids=true, to_apply=%region_13.14.clone | all-reduce | flops 8192 | bytes 65536
  401.6 3.3 reduce-scatter.9.cloned.1.call-done
  406.8 22.6 %all-gather = f32[32,1,128]{2,1,0:T(1,128)S(1)} all-gather(f32[1,1,128]{2,1,0:T(1,128)S(1)} %dynamic-slice_bitcast_fusion), channel_id=1, replica_groups=mesh['group'=4,'shard'=32] {'shard'}, dimensions={0}, use_global_device_ids=true | all-gather | bytes 16896 | tf_op jit(solution)/shard_map/all_gather | solution.py:81
  429.3 20.8 %all-gather.1 = f32[32,1,128]{2,1,0:T(1,128)S(1)} all-gather(f32[1,1,128]{2,1,0:T(1,128)S(1)} %bitcast.89), channel_id=1, replica_groups=mesh['group'=4,'shard'=32] {'shard'}, dimensions={0}, use_global_device_ids=true | all-gather | bytes 16896 | tf_op jit(solution)/shard_map/all_gather | solution.py:80
  450.1 4.9 all-gather.10.cloned.1.call-done
  455.0 12.0 %subtract_multiply_fusion.1 = f32[4096,512]{0,1:T(8,128)S(1)} fusion(f32[4096,256]{1,0:T(8,128)} %all-gather.10.cloned.1.call-done, f32[4096]{0:T(1024)S(1)} %bitcast.87, f32[4096]{0:T(1024)S(1)} %bitcast.85, f32[4096]{0:T(1024)S(1)} %get-tuple-element.8, f32[4096,512]{0,1:T(8,128)} %get-tuple-element.20, f32[2,512,256]{2,1,0:T(8,128)S(1)} %copy-done.8), kind=kOutput, calls=%fused_computation.2 | convolution fusion | flops 6452936704 | bytes 21544960 | tf_op jit(solution)/shard_map/dot_general | solution.py:11
  467.0 3.2 copy-done.2
  470.2 15.4 %convolution_multiply_fusion.1 = f32[4096,256]{1,0:T(8,128)} fusion(f32[4096,512]{0,1:T(8,128)S(1)} %subtract_multiply_fusion.1, f32[2,512,256]{2,1,0:T(8,128)S(1)} %copy-done.8), kind=kOutput, calls=%fused_computation.7 | convolution fusion | flops 6443499520 | bytes 13107200 | tf_op jit(solution)/shard_map/dot_general | solution.py:11
  485.8 20.6 %all-gather.2 = f32[32,1,128]{2,1,0:T(1,128)S(1)} all-gather(f32[1,1,128]{2,1,0:T(1,128)S(1)} %dynamic-slice_bitcast_fusion.1), channel_id=1, replica_groups=mesh['group'=4,'shard'=32] {'shard'}, dimensions={0}, use_global_device_ids=true | all-gather | bytes 16896 | tf_op jit(solution)/shard_map/all_gather | solution.py:81
  506.4 19.8 %all-gather.3 = f32[32,1,128]{2,1,0:T(1,128)S(1)} all-gather(f32[1,1,128]{2,1,0:T(1,128)S(1)} %bitcast.90), channel_id=1, replica_groups=mesh['group'=4,'shard'=32] {'shard'}, dimensions={0}, use_global_device_ids=true | all-gather | bytes 16896 | tf_op jit(solution)/shard_map/all_gather | solution.py:80
  526.2 12.2 %subtract_multiply_fusion = f32[4096,512]{0,1:T(8,128)S(1)} fusion(f32[4096,256]{1,0:T(8,128)} %all-gather.12.cloned.1.call-done, f32[4096]{0:T(1024)S(1)} %bitcast.88, f32[4096]{0:T(1024)S(1)} %bitcast.83, f32[4096]{0:T(1024)S(1)} %get-tuple-element.7, f32[4096,512]{0,1:T(8,128)} %get-tuple-element.18, f32[2,512,256]{2,1,0:T(8,128)S(1)} %copy-done.8), kind=kOutput, calls=%fused_computation | convolution fusion | flops 6452936704 | bytes 21544960 | tf_op jit(solution)/shard_map/dot_general | solution.py:11
  538.4 3.2 copy-done.3
  541.6 15.4 %convolution_multiply_fusion = f32[4096,256]{1,0:T(8,128)} fusion(f32[4096,512]{0,1:T(8,128)S(1)} %subtract_multiply_fusion, f32[2,512,256]{2,1,0:T(8,128)S(1)} %copy-done.8), kind=kOutput, calls=%fused_computation.6 | convolution fusion | flops 6443499520 | bytes 13107200 | tf_op jit(solution)/shard_map/dot_general | solution.py:11
  557.0 10.3 %convolution_multiply_fusion.3 = f32[512,256]{1,0:T(8,128)S(1)} fusion(f32[4096,512]{0,1:T(8,128)} %copy-done.2, f32[4096,256]{1,0:T(8,128)} %bitcast.78), kind=kOutput, calls=%fused_computation.21 | convolution fusion | flops 6442582016 | bytes 13107200 | tf_op jit(solution)/shard_map/dot_general | solution.py:11
  567.4 6.7 convolution_multiply_fusion.2
  574.1 8.1 fusion.17
  582.2 3.8 reduce-scatter.7.cloned.1.call-done
  586.9 84.4 %reduce-scatter.11.cloned.1.call-done = f32[128,256]{1,0:T(8,128)} async-done(((f32[4096,256]{1,0:T(8,128)}), f32[128,256]{1,0:T(8,128)}) %reduce-scatter.11.cloned.1.call-update) | async-done | bytes 131088 | tf_op jit(solution)/shard_map/reduce_scatter | solution.py:87
  672.9 4.1 all-to-all-start.2
  677.1 10.9 %fusion.23 = f32[1,512,256]{2,1,0:T(8,128)S(1)} fusion(f32[512,256]{1,0:T(8,128)S(1)} %convolution_multiply_fusion.2, f32[4096,256]{1,0:T(8,128)} %all-gather.12.cloned.1.call-done, f32[4096,512]{0,1:T(8,128)} %get-tuple-element.18, f32[4096]{0:T(1024)S(1)} %bitcast.84, f32[4096]{0:T(1024)S(1)} %get-tuple-element.7), kind=kOutput, calls=%fused_computation.25 | convolution fusion | flops 6448873472 | bytes 13664256 | tf_op jit(solution)/shard_map/dot_general | solution.py:11
  690.4 140.6 %all-reduce.6.cloned.1.call-done = f32[64,256]{1,0:T(8,128)} async-done(((f32[64,256]{1,0:T(8,128)}), f32[64,256]{1,0:T(8,128)}) %all-reduce.6.cloned.1.call-update) | async-done | bytes 65552 | tf_op jit(solution)/shard_map/psum | solution.py:96
  (85 shorter events, 18.4 us)
Async XLA Ops:
  7.2 1.9 copy-start
  7.2 68.8 %all-gather.8.cloned.1.call-start = ((), (), s32[]{:S(2)}) async-start(), calls=%async_computation.7 | async-start | bytes 8650752 | tf_op jit(solution)/shard_map/all_gather | solution.py:58
  21.8 58.5 %copy-start.8 = (f32[2,512,256]{2,1,0:T(8,128)S(1)}, f32[2,512,256]{2,1,0:T(8,128)}, u32[]{:S(2)}) copy-start(f32[2,512,256]{2,1,0:T(8,128)} %param.7) | copy-start | bytes 3145732
  21.9 377.8 %reduce-scatter.5.cloned.1.call-start = ((), (), s32[]{:S(2)}) async-start(), calls=%async_computation.8 | async-start | bytes 4325376 | tf_op jit(solution)/shard_map/reduce_scatter | solution.py:72
  80.3 9.3 %copy-start.5 = (f32[1,128,32,256]{3,2,0,1:T(8,128)}, f32[1,128,32,256]{3,2,0,1:T(8,128)S(1)}, u32[]{:S(2)}) copy-start(f32[1,128,32,256]{3,2,0,1:T(8,128)S(1)} %get-tuple-element.14) | copy-start | bytes 12582916
  80.3 9.3 %copy-start.7 = (f32[1,128,32,256]{3,2,0,1:T(8,128)}, f32[1,128,32,256]{3,2,0,1:T(8,128)S(1)}, u32[]{:S(2)}) copy-start(f32[1,128,32,256]{3,2,0,1:T(8,128)S(1)} %get-tuple-element.13) | copy-start | bytes 12582916
  237.3 167.6 %reduce-scatter.9.cloned.1.call-start = ((), (), s32[]{:S(2)}) async-start(), calls=%async_computation.11 | async-start | bytes 4325376 | tf_op jit(solution)/shard_map/reduce_scatter | solution.py:72
  237.6 22.2 %copy-start.15 = (u32[128]{0:T(128)S(1)}, u32[128]{0:T(128)}, u32[]{:S(2)}) copy-start(u32[128]{0:T(128)} %constant.59) | copy-start | bytes 1540
  237.6 26.4 %copy-start.9 = (f32[2,4,32,256]{3,2,0,1:T(8,128)S(1)}, f32[2,4,32,256]{3,2,0,1:T(8,128)}, u32[]{:S(2)}) copy-start(f32[2,4,32,256]{3,2,0,1:T(8,128)} %all_to_all.15) | copy-start | bytes 786436
  255.7 8.3 all-to-all-start.1
  259.8 195.2 %all-gather.10.cloned.1.call-start = ((), (), s32[]{:S(2)}) async-start(), calls=%async_computation.9 | async-start | bytes 4325376 | tf_op jit(solution)/shard_map/all_gather | solution.py:79
  401.4 124.8 %all-gather.12.cloned.1.call-start = ((), (), s32[]{:S(2)}) async-start(), calls=%async_computation.12 | async-start | bytes 4325376 | tf_op jit(solution)/shard_map/all_gather | solution.py:79
  406.6 179.4 %reduce-scatter.7.cloned.1.call-start = ((), (), s32[]{:S(2)}) async-start(), calls=%async_computation.10 | async-start | bytes 4325376 | tf_op jit(solution)/shard_map/reduce_scatter | solution.py:87
  467.0 3.2 copy-start.2
  485.6 185.6 %reduce-scatter.11.cloned.1.call-start = ((), (), s32[]{:S(2)}) async-start(), calls=%async_computation.13 | async-start | bytes 4325376 | tf_op jit(solution)/shard_map/reduce_scatter | solution.py:87
  538.4 3.2 copy-start.3
  557.0 10.3 %copy-start.4 = (f32[4096,512]{0,1:T(8,128)S(1)}, f32[4096,512]{0,1:T(8,128)}, u32[]{:S(2)}) copy-start(f32[4096,512]{0,1:T(8,128)} %copy-done.3) | copy-start | bytes 25165828
  557.0 10.3 %copy-start.6 = (f32[1,128,32,256]{3,2,0,1:T(8,128)S(1)}, f32[1,128,32,256]{3,2,0,1:T(8,128)}, u32[]{:S(2)}) copy-start(f32[1,128,32,256]{3,2,0,1:T(8,128)} %copy-done.5) | copy-start | bytes 12582916
  557.0 17.1 %slice-start = ((s8[8388608]{0:T(1024)(128)(4,1)}), s8[4194304]{0:T(1024)(128)(4,1)S(1)}, s32[]{:S(2)}) async-start(s8[8388608]{0:T(1024)(128)(4,1)} %bitcast.73), calls=%async_computation.15 | async-start | bytes 8388608
  567.3 6.7 slice-start.1
  567.4 6.7 copy-start.14
  574.1 11.9 %copy-start.10 = (f32[128,256]{1,0:T(8,128)S(1)}, f32[128,256]{1,0:T(8,128)}, u32[]{:S(2)}) copy-start(f32[128,256]{1,0:T(8,128)} %get-tuple-element.10) | copy-start | bytes 393220
  574.1 97.2 %copy-start.11 = (f32[128,256]{1,0:T(8,128)S(1)}, f32[128,256]{1,0:T(8,128)}, u32[]{:S(2)}) copy-start(f32[128,256]{1,0:T(8,128)} %get-tuple-element.12) | copy-start | bytes 393220
  672.9 15.1 %all-to-all-start.2 = ((f32[2,4,32,256]{3,2,0,1:T(8,128)}), f32[2,4,32,256]{3,2,0,1:T(8,128)S(1)}, u32[]{:S(2)}, u32[]{:S(2)}) async-start(f32[2,4,32,256]{3,2,0,1:T(8,128)} %pad_maximum_fusion.1), calls=%async_computation.6 | async-start | bytes 524288 | tf_op jit(solution)/shard_map/all_to_all | solution.py:94
  677.1 11.3 %copy-start.13 = (s32[128]{0:T(128)S(1)}, s32[128]{0:T(128)}, u32[]{:S(2)}) copy-start(s32[128]{0:T(128)} %param.5) | copy-start | bytes 1540
  677.1 153.9 %all-reduce.6.cloned.1.call-start = ((), (), s32[]{:S(2)}) async-start(), calls=%async_computation.14 | async-start | bytes 131072 | tf_op jit(solution)/shard_map/psum | solution.py:96
  677.1 155.4 %copy-start.1 = (f32[64,256]{1,0:T(8,128)S(1)}, f32[64,256]{1,0:T(8,128)}, u32[]{:S(2)}) copy-start(f32[64,256]{1,0:T(8,128)} %param.6) | copy-start | bytes 196612
  688.4 144.1 %copy-start.12 = (f32[128,256]{1,0:T(8,128)}, f32[128,256]{1,0:T(8,128)S(1)}, u32[]{:S(2)}) copy-start(f32[128,256]{1,0:T(8,128)S(1)} %fusion.46) | copy-start | bytes 393220
Sparse Core Ops, SparseCore 0:
  22.0 53.9 all-gather.7
  237.5 82.1 reduce-scatter.4
  323.3 81.6 reduce-scatter.8
  407.6 47.2 all-gather.9
  457.6 45.2 all-gather.11
  506.4 79.4 reduce-scatter.6
  589.6 81.6 reduce-scatter.10
  689.5 141.5 all-reduce.5
where the time goes:
time: 847 us; the launch traced here: 840 us
  blocking collectives  342 us (40%)
  waiting for transfers between devices  294 us (35%)
  matrix products  146 us (17%)
  other arithmetic  18.8 us (2%)
  between operations  15.6 us (2%)
  local copies, waits for them, and re-layouts  14.2 us (2%)
  starting transfers between devices  8.75 us (1%)
    dot_general x16, matrix products, contract(): lax.dot_general(former, latter, (((former_dim,), (latter_dim,)), ((), ())...  146 us
    psum x1, waiting for transfers between devices, per_device(): lax.psum(-contract(onehot, item_grad, 0, 0), ('group', 'shard'))  141 us
    unnamed x1, blocking collectives  126 us
    pmax x1, blocking collectives, per_device(): peak_score = lax.pmax(jnp.max(scores, axis=1), 'shard')  121 us
    reduce_scatter x2, waiting for transfers between devices, per_device(): lax.psum_scatter(pushed, 'shard', scatter_dimension=0, tiled=True)  88.1 us
    all_gather x1, waiting for transfers between devices, per_device(): lax.all_gather(arrived, 'shard', axis=1, tiled=True)  54.1 us
    all_gather x2, blocking collectives, per_device(): lax.all_gather(denominator_own, 'shard', axis=0, tiled=True)  43.2 us
    all_gather x2, blocking collectives, per_device(): lax.all_gather(own_inner, 'shard', axis=0, tiled=True)  40.5 us
  transfers between devices with their start and end apart: 10, of which 7 were waited for; matrix products, arithmetic and copies ran while one was open for 15% of the time, Pallas kernels for 0%

commit v1 on v0

--- a/solution.py
+++ b/solution.py
@@ -5,6 +5,12 @@
 
 sharpness = 2.5
 highest = lax.Precision.HIGHEST
+
+
+def gather_and_add(value, axis):
+    parts = lax.all_gather(value, axis, axis=0, tiled=False)
+    total = parts.sum(axis=0)
+    return total
 
 
 def contract(former, latter, former_dim, latter_dim):
@@ -93,7 +99,7 @@
     returned = jnp.stack(row_grads).reshape(local_groups, group_count, slot_size, feature_count)
     homeward = lax.all_to_all(returned, "group", split_axis=1, concat_axis=1, tiled=True)
     item_grad = contract(placing, homeward.reshape(slot_total, feature_count), 0, 0)
-    coarse_grad = lax.psum(-contract(onehot, item_grad, 0, 0), ("group", "shard"))
+    coarse_grad = gather_and_add(-contract(onehot, item_grad, 0, 0), ("group", "shard"))
     return (item_grad, fine_grad, coarse_grad)
 
 

time: 847 us -> 773 us (0.913)
  waiting for transfers between devices: 294 us -> 213 us
  blocking collectives: 342 us -> 352 us
    psum x1 -> x0, waiting for transfers between devices: 141 us -> none  [per_device(): lax.psum(-contract(onehot, item_grad, 0, 0), ('group', 'shard'))]
    all_gather x0 -> x1, waiting for transfers between devices: none -> 33.8 us  [gather_and_add(): parts = lax.all_gather(value, axis, axis=0, tiled=False)]
    reduce_scatter x2, waiting for transfers between devices: 88.1 us -> 113 us  [per_device(): lax.psum_scatter(pushed, 'shard', scatter_dimension=0, tiled=True)]
    all_to_all x0 -> x1, blocking collectives: none -> 9.63 us  [per_device(): lax.all_to_all(returned, 'group', split_axis=1, concat_axis=1, tiled=True)]
  transfers between devices with their start and end apart: 10 -> 9, of which waited for: 7 -> 7; matrix products, arithmetic and copies ran while one was open for 15% -> 16% of each run, Pallas kernels for 0% -> 0%
where the time goes in v1:
time: 773 us; the launch traced here: 766 us
  blocking collectives  352 us (46%)
  waiting for transfers between devices  213 us (28%)
  matrix products  146 us (19%)
  other arithmetic  22.6 us (3%)
  between operations  15.4 us (2%)
  local copies, waits for them, and re-layouts  12.7 us (2%)
    dot_general x16, matrix products, contract(): lax.dot_general(former, latter, (((former_dim,), (latter_dim,)), ((), ())...  146 us
    unnamed x1, blocking collectives  126 us
    pmax x1, blocking collectives, per_device(): peak_score = lax.pmax(jnp.max(scores, axis=1), 'shard')  122 us
    reduce_scatter x2, waiting for transfers between devices, per_device(): lax.psum_scatter(pushed, 'shard', scatter_dimension=0, tiled=True)  113 us
    all_gather x1, waiting for transfers between devices, per_device(): lax.all_gather(arrived, 'shard', axis=1, tiled=True)  54.1 us
    all_gather x2, blocking collectives, per_device(): lax.all_gather(denominator_own, 'shard', axis=0, tiled=True)  43.2 us
    all_gather x2, blocking collectives, per_device(): lax.all_gather(own_inner, 'shard', axis=0, tiled=True)  40.5 us
    all_gather x1, waiting for transfers between devices, gather_and_add(): parts = lax.all_gather(value, axis, axis=0, tiled=False)  33.8 us
  transfers between devices with their start and end apart: 9, of which 7 were waited for; matrix products, arithmetic and copies ran while one was open for 16% of the time, Pallas kernels for 0%

profile of v1, /device:TPU:1, one launch (start us, length us, event | category | flops | bytes accessed | tf_op | source)
XLA Modules:
  0.0 766.0 jit_solution(13480117153895938123)
XLA Ops:
  10.5 11.3 %all_to_all.15 = f32[2,4,32,256]{3,2,0,1:T(8,128)} all-to-all(f32[2,4,32,256]{3,2,0,1:T(8,128)S(1)} %copy.28), channel_id=1, replica_groups=mesh['group'=4,'shard'=32] {'group'}, dimensions={1} | all-to-all | bytes 524288 | tf_op jit(solution)/shard_map/all_to_all | solution.py:55
  21.9 54.1 %all-gather.10.cloned.1.call-done = f32[2,128,32,256]{3,2,0,1:T(8,128)} async-done(((f32[2,4,32,256]{3,2,0,1:T(8,128)}), f32[2,128,32,256]{3,2,0,1:T(8,128)}) %all-gather.10.cloned.1.call-update) | async-done | bytes 8388624 | tf_op jit(solution)/shard_map/all_gather | solution.py:64
  76.0 4.4 fusion.61
  80.4 9.3 %multiply_reduce_fusion = (f32[4096]{0:T(1024)S(1)}, f32[4096,512]{0,1:T(8,128)}) fusion(f32[4096,256]{1,0:T(8,128)S(1)} %bitcast.78, f32[2,512,256]{2,1,0:T(8,128)S(1)} %copy-done.7), kind=kOutput, calls=%fused_computation.4 | convolution fusion | flops 6446641152 | bytes 13123584 | tf_op jit(solution)/shard_map/dot_general | solution.py:17
  89.6 9.2 %multiply_reduce_fusion.1 = (f32[4096]{0:T(1024)S(1)}, f32[4096,512]{0,1:T(8,128)}) fusion(f32[4096,256]{1,0:T(8,128)S(1)} %bitcast.80, f32[2,512,256]{2,1,0:T(8,128)S(1)} %copy-done.7), kind=kOutput, calls=%fused_computation.5 | convolution fusion | flops 6446641152 | bytes 13123584 | tf_op jit(solution)/shard_map/dot_general | solution.py:17
  98.8 121.7 %all-reduce.3 = (f32[4096]{0:T(1024)S(1)}, f32[4096]{0:T(1024)S(1)}) all-reduce(f32[4096]{0:T(1024)S(1)} %get-tuple-element.17, f32[4096]{0:T(1024)S(1)} %get-tuple-element.19), channel_id=1, replica_groups=mesh['group'=4,'shard'=32] {'shard'}, use_global_device_ids=true, to_apply=%region_11.12 | all-reduce | flops 8192 | bytes 65536 | tf_op jit(solution)/shard_map/pmax | solution.py:73
  220.5 17.2 %fusion = f32[4096,256]{1,0:T(8,128)} fusion(f32[4096,512]{0,1:T(8,128)} %get-tuple-element.20, f32[4096]{0:T(1024)S(1)} %get-tuple-element.8, f32[2,512,256]{2,1,0:T(8,128)S(1)} %copy-done.7), kind=kOutput, calls=%fused_computation.8 | convolution fusion | flops 6446645248 | bytes 13123584 | tf_op jit(solution)/shard_map/dot_general | solution.py:17
  238.0 17.2 %fusion.3 = f32[4096,256]{1,0:T(8,128)} fusion(f32[4096,512]{0,1:T(8,128)} %get-tuple-element.18, f32[4096]{0:T(1024)S(1)} %get-tuple-element.7, f32[2,512,256]{2,1,0:T(8,128)S(1)} %copy-done.7), kind=kOutput, calls=%fused_computation.11 | convolution fusion | flops 6446645248 | bytes 13123584 | tf_op jit(solution)/shard_map/dot_general | solution.py:17
  256.0 4.1 all-to-all-start.1
  264.4 5.0 fusion.2
  269.4 5.0 fusion.5
  274.4 125.5 %all-reduce.2 = (f32[4096]{0:T(1024)S(1)}, f32[4096]{0:T(1024)S(1)}) all-reduce(f32[4096]{0:T(1024)S(1)} %fusion.5, f32[4096]{0:T(1024)S(1)} %fusion.2), channel_id=6, replica_groups=mesh['group'=4,'shard'=32] {'shard'}, use_global_device_ids=true, to_apply=%region_13.14.clone | all-reduce | flops 8192 | bytes 65536
  401.9 3.5 reduce-scatter.9.cloned.1.call-done
  407.2 22.6 %all-gather.1 = f32[32,1,128]{2,1,0:T(1,128)S(1)} all-gather(f32[1,1,128]{2,1,0:T(1,128)S(1)} %dynamic-slice_bitcast_fusion), channel_id=1, replica_groups=mesh['group'=4,'shard'=32] {'shard'}, dimensions={0}, use_global_device_ids=true | all-gather | bytes 16896 | tf_op jit(solution)/shard_map/all_gather | solution.py:87
  429.7 20.6 %all-gather.2 = f32[32,1,128]{2,1,0:T(1,128)S(1)} all-gather(f32[1,1,128]{2,1,0:T(1,128)S(1)} %bitcast.93), channel_id=1, replica_groups=mesh['group'=4,'shard'=32] {'shard'}, dimensions={0}, use_global_device_ids=true | all-gather | bytes 16896 | tf_op jit(solution)/shard_map/all_gather | solution.py:86
  450.3 5.1 all-gather.12.cloned.1.call-done
  455.4 12.0 %subtract_multiply_fusion.1 = f32[4096,512]{0,1:T(8,128)S(1)} fusion(f32[4096,256]{1,0:T(8,128)} %all-gather.12.cloned.1.call-done, f32[4096]{0:T(1024)S(1)} %bitcast.91, f32[4096]{0:T(1024)S(1)} %bitcast.87, f32[4096]{0:T(1024)S(1)} %get-tuple-element.8, f32[4096,512]{0,1:T(8,128)} %get-tuple-element.20, f32[2,512,256]{2,1,0:T(8,128)S(1)} %copy-done.7), kind=kOutput, calls=%fused_computation.2 | convolution fusion | flops 6452936704 | bytes 21544960 | tf_op jit(solution)/shard_map/dot_general | solution.py:17
  467.4 3.2 copy-done.2
  470.6 15.4 %convolution_multiply_fusion.1 = f32[4096,256]{1,0:T(8,128)} fusion(f32[4096,512]{0,1:T(8,128)S(1)} %subtract_multiply_fusion.1, f32[2,512,256]{2,1,0:T(8,128)S(1)} %copy-done.7), kind=kOutput, calls=%fused_computation.7 | convolution fusion | flops 6443499520 | bytes 13107200 | tf_op jit(solution)/shard_map/dot_general | solution.py:17
  486.2 20.7 %all-gather.3 = f32[32,1,128]{2,1,0:T(1,128)S(1)} all-gather(f32[1,1,128]{2,1,0:T(1,128)S(1)} %dynamic-slice_bitcast_fusion.1), channel_id=1, replica_groups=mesh['group'=4,'shard'=32] {'shard'}, dimensions={0}, use_global_device_ids=true | all-gather | bytes 16896 | tf_op jit(solution)/shard_map/all_gather | solution.py:87
  506.9 20.0 %all-gather.4 = f32[32,1,128]{2,1,0:T(1,128)S(1)} all-gather(f32[1,1,128]{2,1,0:T(1,128)S(1)} %bitcast.94), channel_id=1, replica_groups=mesh['group'=4,'shard'=32] {'shard'}, dimensions={0}, use_global_device_ids=true | all-gather | bytes 16896 | tf_op jit(solution)/shard_map/all_gather | solution.py:86
  526.9 12.2 %subtract_multiply_fusion = f32[4096,512]{0,1:T(8,128)S(1)} fusion(f32[4096,256]{1,0:T(8,128)} %all-gather.14.cloned.1.call-done, f32[4096]{0:T(1024)S(1)} %bitcast.92, f32[4096]{0:T(1024)S(1)} %bitcast.89, f32[4096]{0:T(1024)S(1)} %get-tuple-element.7, f32[4096,512]{0,1:T(8,128)} %get-tuple-element.18, f32[2,512,256]{2,1,0:T(8,128)S(1)} %copy-done.7), kind=kOutput, calls=%fused_computation | convolution fusion | flops 6452936704 | bytes 21544960 | tf_op jit(solution)/shard_map/dot_general | solution.py:17
  542.3 15.4 %convolution_multiply_fusion = f32[4096,256]{1,0:T(8,128)} fusion(f32[4096,512]{0,1:T(8,128)S(1)} %subtract_multiply_fusion, f32[2,512,256]{2,1,0:T(8,128)S(1)} %copy-done.7), kind=kOutput, calls=%fused_computation.6 | convolution fusion | flops 6443499520 | bytes 13107200 | tf_op jit(solution)/shard_map/dot_general | solution.py:17
  557.8 28.7 %reduce-scatter.7.cloned.1.call-done = f32[128,256]{1,0:T(8,128)} async-done(((f32[4096,256]{1,0:T(8,128)}), f32[128,256]{1,0:T(8,128)}) %reduce-scatter.7.cloned.1.call-update) | async-done | bytes 131088 | tf_op jit(solution)/shard_map/reduce_scatter | solution.py:93
  587.4 84.4 %reduce-scatter.11.cloned.1.call-done = f32[128,256]{1,0:T(8,128)} async-done(((f32[4096,256]{1,0:T(8,128)}), f32[128,256]{1,0:T(8,128)}) %reduce-scatter.11.cloned.1.call-update) | async-done | bytes 131088 | tf_op jit(solution)/shard_map/reduce_scatter | solution.py:93
  672.7 9.6 %all_to_all.16 = f32[2,4,32,256]{3,2,0,1:T(8,128)S(1)} all-to-all(f32[2,4,32,256]{3,2,0,1:T(8,128)S(1)} %pad_maximum_fusion.1), channel_id=1, replica_groups=mesh['group'=4,'shard'=32] {'group'}, dimensions={1} | all-to-all | bytes 524288 | tf_op jit(solution)/shard_map/all_to_all | solution.py:100
  683.7 10.0 %convolution_multiply_fusion.3 = f32[512,256]{1,0:T(8,128)S(1)} fusion(f32[4096,512]{0,1:T(8,128)} %copy-done.2, f32[4096,256]{1,0:T(8,128)} %bitcast.81), kind=kOutput, calls=%fused_computation.21 | convolution fusion | flops 6442582016 | bytes 13107200 | tf_op jit(solution)/shard_map/dot_general | solution.py:17
  693.7 9.9 %convolution_multiply_fusion.2 = f32[512,256]{1,0:T(8,128)S(1)} fusion(f32[4096,512]{0,1:T(8,128)} %copy-done.3, f32[4096,256]{1,0:T(8,128)S(1)} %bitcast.79), kind=kOutput, calls=%fused_computation.20 | convolution fusion | flops 6442582016 | bytes 13107200 | tf_op jit(solution)/shard_map/dot_general | solution.py:17
  703.7 7.8 %fusion.17 = f32[1,512,256]{2,1,0:T(8,128)S(1)} fusion(f32[512,256]{1,0:T(8,128)S(1)} %convolution_multiply_fusion.3, f32[4096,256]{1,0:T(8,128)S(1)} %copy-done.13, f32[4096,512]{0,1:T(8,128)S(1)} %bitcast.77, f32[4096]{0:T(1024)S(1)} %bitcast.88, f32[4096]{0:T(1024)S(1)} %get-tuple-element.8), kind=kOutput, calls=%fused_computation.23 | convolution fusion | flops 6448873472 | bytes 13664256 | tf_op jit(solution)/shard_map/dot_general | solution.py:17
  711.6 8.1 %fusion.23 = f32[1,512,256]{2,1,0:T(8,128)S(1)} fusion(f32[512,256]{1,0:T(8,128)S(1)} %convolution_multiply_fusion.2, f32[4096,256]{1,0:T(8,128)S(1)} %copy-done.14, f32[4096,512]{0,1:T(8,128)S(1)} %bitcast.75, f32[4096]{0:T(1024)S(1)} %bitcast.90, f32[4096]{0:T(1024)S(1)} %get-tuple-element.7), kind=kOutput, calls=%fused_computation.25 | convolution fusion | flops 6448873472 | bytes 13664256 | tf_op jit(solution)/shard_map/dot_general | solution.py:17
  720.7 33.8 %all-gather.16.cloned.1.call-done = f32[8192,256]{1,0:T(8,128)} async-done(((f32[64,256]{1,0:T(8,128)}), f32[8192,256]{1,0:T(8,128)}) %all-gather.16.cloned.1.call-update) | async-done | bytes 8388624 | tf_op jit(solution)/shard_map/all_gather | solution.py:11
  754.5 4.5 reduce_sum.69
  (89 shorter events, 19.4 us)
Async XLA Ops:
  7.2 1.9 copy-start
  7.2 68.8 %all-gather.10.cloned.1.call-start = ((), (), s32[]{:S(2)}) async-start(), calls=%async_computation.7 | async-start | bytes 8650752 | tf_op jit(solution)/shard_map/all_gather | solution.py:64
  21.8 58.5 %copy-start.7 = (f32[2,512,256]{2,1,0:T(8,128)S(1)}, f32[2,512,256]{2,1,0:T(8,128)}, u32[]{:S(2)}) copy-start(f32[2,512,256]{2,1,0:T(8,128)} %param.7) | copy-start | bytes 3145732
  21.8 378.2 %reduce-scatter.5.cloned.1.call-start = ((), (), s32[]{:S(2)}) async-start(), calls=%async_computation.8 | async-start | bytes 4325376 | tf_op jit(solution)/shard_map/reduce_scatter | solution.py:78
  80.3 9.3 %copy-start.4 = (f32[1,128,32,256]{3,2,0,1:T(8,128)}, f32[1,128,32,256]{3,2,0,1:T(8,128)S(1)}, u32[]{:S(2)}) copy-start(f32[1,128,32,256]{3,2,0,1:T(8,128)S(1)} %get-tuple-element.14) | copy-start | bytes 12582916
  80.3 9.3 %copy-start.6 = (f32[1,128,32,256]{3,2,0,1:T(8,128)}, f32[1,128,32,256]{3,2,0,1:T(8,128)S(1)}, u32[]{:S(2)}) copy-start(f32[1,128,32,256]{3,2,0,1:T(8,128)S(1)} %get-tuple-element.13) | copy-start | bytes 12582916
  237.7 167.6 %reduce-scatter.9.cloned.1.call-start = ((), (), s32[]{:S(2)}) async-start(), calls=%async_computation.11 | async-start | bytes 4325376 | tf_op jit(solution)/shard_map/reduce_scatter | solution.py:78
  238.0 22.2 %copy-start.15 = (u32[128]{0:T(128)S(1)}, u32[128]{0:T(128)}, u32[]{:S(2)}) copy-start(u32[128]{0:T(128)} %constant.59) | copy-start | bytes 1540
  238.0 26.4 %copy-start.8 = (f32[2,4,32,256]{3,2,0,1:T(8,128)S(1)}, f32[2,4,32,256]{3,2,0,1:T(8,128)}, u32[]{:S(2)}) copy-start(f32[2,4,32,256]{3,2,0,1:T(8,128)} %all_to_all.15) | copy-start | bytes 786436
  256.0 8.3 %all-to-all-start.1 = ((f32[2,4,32]{2,0,1:T(2,128)}), f32[2,4,32]{2,0,1:T(2,128)S(1)}, u32[]{:S(2)}, u32[]{:S(2)}) async-start(f32[2,4,32]{2,0,1:T(2,128)} %copy.29), calls=%async_computation.2 | async-start | bytes 8192 | tf_op jit(solution)/shard_map/all_to_all | solution.py:56
  260.2 195.2 %all-gather.12.cloned.1.call-start = ((), (), s32[]{:S(2)}) async-start(), calls=%async_computation.9 | async-start | bytes 4325376 | tf_op jit(solution)/shard_map/all_gather | solution.py:85
  401.7 125.2 %all-gather.14.cloned.1.call-start = ((), (), s32[]{:S(2)}) async-start(), calls=%async_computation.12 | async-start | bytes 4325376 | tf_op jit(solution)/shard_map/all_gather | solution.py:85
  407.1 179.4 %reduce-scatter.7.cloned.1.call-start = ((), (), s32[]{:S(2)}) async-start(), calls=%async_computation.10 | async-start | bytes 4325376 | tf_op jit(solution)/shard_map/reduce_scatter | solution.py:93
  467.4 3.2 copy-start.2
  486.1 185.7 %reduce-scatter.11.cloned.1.call-start = ((), (), s32[]{:S(2)}) async-start(), calls=%async_computation.13 | async-start | bytes 4325376 | tf_op jit(solution)/shard_map/reduce_scatter | solution.py:93
  539.1 3.2 copy-start.3
  542.3 44.2 %copy-start.9 = (f32[128,256]{1,0:T(8,128)S(1)}, f32[128,256]{1,0:T(8,128)}, u32[]{:S(2)}) copy-start(f32[128,256]{1,0:T(8,128)} %get-tuple-element.10) | copy-start | bytes 393220
  542.3 129.5 %copy-start.10 = (f32[128,256]{1,0:T(8,128)S(1)}, f32[128,256]{1,0:T(8,128)}, u32[]{:S(2)}) copy-start(f32[128,256]{1,0:T(8,128)} %get-tuple-element.12) | copy-start | bytes 393220
  542.3 140.4 %copy-start.12 = (s32[128]{0:T(128)S(1)}, s32[128]{0:T(128)}, u32[]{:S(2)}) copy-start(s32[128]{0:T(128)} %param.5) | copy-start | bytes 1540
  557.7 196.8 %all-gather.16.cloned.1.call-start = ((), (), s32[]{:S(2)}) async-start(), calls=%async_computation.14 | async-start | bytes 8454144 | tf_op jit(solution)/shard_map/all_gather | solution.py:11
  682.7 11.0 %copy-start.11 = (f32[128,256]{1,0:T(8,128)}, f32[128,256]{1,0:T(8,128)S(1)}, u32[]{:S(2)}) copy-start(f32[128,256]{1,0:T(8,128)S(1)} %fusion.46) | copy-start | bytes 393220
  683.7 10.0 %copy-start.5 = (f32[1,128,32,256]{3,2,0,1:T(8,128)S(1)}, f32[1,128,32,256]{3,2,0,1:T(8,128)}, u32[]{:S(2)}) copy-start(f32[1,128,32,256]{3,2,0,1:T(8,128)} %copy-done.4) | copy-start | bytes 12582916
  683.7 20.0 %slice-start.2 = ((s8[8388608]{0:T(1024)(128)(4,1)}), s8[4194304]{0:T(1024)(128)(4,1)S(1)}, s32[]{:S(2)}) async-start(s8[8388608]{0:T(1024)(128)(4,1)} %bitcast.76), calls=%async_computation.17 | async-start | bytes 8388608
  693.7 10.0 %slice-start.3 = ((s8[8388608]{0:T(1024)(128)(4,1)}), s8[4194304]{0:T(1024)(128)(4,1)S(1)}, s32[]{:S(2)}) async-start(s8[8388608]{0:T(1024)(128)(4,1)} %bitcast.76), calls=%async_computation.18 | async-start | bytes 8388608
  693.7 10.0 %copy-start.13 = (f32[4096,256]{1,0:T(8,128)S(1)}, f32[4096,256]{1,0:T(8,128)}, u32[]{:S(2)}) copy-start(f32[4096,256]{1,0:T(8,128)} %all-gather.12.cloned.1.call-done) | copy-start | bytes 12582916
  693.7 17.8 %slice-start = ((s8[8388608]{0:T(1024)(128)(4,1)}), s8[4194304]{0:T(1024)(128)(4,1)S(1)}, s32[]{:S(2)}) async-start(s8[8388608]{0:T(1024)(128)(4,1)} %bitcast.74), calls=%async_computation.15 | async-start | bytes 8388608
  703.7 7.8 %slice-start.1 = ((s8[8388608]{0:T(1024)(128)(4,1)}), s8[4194304]{0:T(1024)(128)(4,1)S(1)}, s32[]{:S(2)}) async-start(s8[8388608]{0:T(1024)(128)(4,1)} %bitcast.74), calls=%async_computation.16 | async-start | bytes 8388608
  703.7 7.8 %copy-start.14 = (f32[4096,256]{1,0:T(8,128)S(1)}, f32[4096,256]{1,0:T(8,128)}, u32[]{:S(2)}) copy-start(f32[4096,256]{1,0:T(8,128)} %all-gather.14.cloned.1.call-done) | copy-start | bytes 12582916
  711.6 47.4 %copy-start.1 = (f32[64,256]{1,0:T(8,128)S(1)}, f32[64,256]{1,0:T(8,128)}, u32[]{:S(2)}) copy-start(f32[64,256]{1,0:T(8,128)} %param.6) | copy-start | bytes 196612
Sparse Core Ops, SparseCore 0:
  22.0 53.9 all-gather.9
  237.9 82.1 reduce-scatter.4
  323.7 81.6 reduce-scatter.8
  408.1 47.2 all-gather.11
  458.1 45.2 all-gather.13
  506.9 79.5 reduce-scatter.6
  590.1 81.6 reduce-scatter.10
  683.8 70.6 all-gather.15
